TPU v7x, 32 devices: a whole 2x2x4 slice. The times are simulated.
32 devices in a mesh: groups: 2 (over y), tm: 8 (over z, x), space: 2 (over core).
Axes of the slice: x: 2, y: 2, z: 4, core: 2. Of those that a mesh axis runs over, the one named last changes fastest.
Arguments:
- latent: bfloat16 [32, 16, 32, 256], P(('groups', 'tm'), 'space'), parts along dimension 0, may hold values from -6 to 6
- first_kernel: bfloat16 [256, 27, 256], P('tm'), may hold values from -0.078125 to 0.078125
- second_kernel: bfloat16 [256, 27, 128], P('tm'), may hold values from -0.078125 to 0.078125
Outputs:
- decoded: bfloat16 [32, 32, 64, 128], P(('groups', 'tm'), 'space'), parts along dimension 0
There are 2 independent parts, one for each index of `groups`. A program takes and returns all parts, laid end to end along the dimension named above; an argument that names none is the same for every part. Nothing has to cross between parts.
All inputs are finite; a program needn't handle non-finite values.
Results may differ from a plain program's by a relative error of at most 0.005.
Values may be sent and summed in bfloat16 or wider, within the bound.
A program may use at most 64 MiB of HBM per device.

v0:
```python
import jax
import jax.numpy as jnp
from jax import lax
from jax.sharding import PartitionSpec as P


def shifted(x, axis, by):
    count = lax.axis_size(axis)
    pairs = [(i, i + by) for i in range(count) if 0 <= i + by < count]
    return lax.ppermute(x, axis, pairs)


def padded_2(x, sides, width):
    for axis, dim in sides:
        count, length = (lax.axis_size(axis), x.shape[dim])
        up = [(i, (i + 1) % count) for i in range(count - 1)]
        down = [(j, i) for i, j in up]
        last = lax.slice_in_dim(x, length - width, length, axis=dim)
        leading = lax.slice_in_dim(x, 0, width, axis=dim)
        before = lax.ppermute(last, axis, up)
        after = lax.ppermute(leading, axis, down)
        x = jnp.concatenate([before, x, after], axis=dim)
    return x


def conv_block(padded, kernel):
    channels = kernel.shape[0]
    outputs = kernel.shape[2]
    filters = kernel.reshape(channels, 3, 3, 3, outputs).transpose(1, 2, 3, 0, 4)
    result = lax.conv_general_dilated(
        padded[None],
        filters,
        (1, 1, 1),
        ((0, 0), (0, 0), (1, 1)),
        dimension_numbers=("NDHWC", "DHWIO", "NDHWC"),
        preferred_element_type=jnp.float32,
    )
    return result[0]


def upsample(field):
    return jnp.repeat(jnp.repeat(field, 2, axis=1), 2, axis=2)


def shards(latent, first_kernel, second_kernel):
    frames = latent.shape[0]
    past = shifted(latent, "tm", 1)
    extended = jnp.concatenate([past, latent], 0)
    padded = padded_2(extended, (("space", 1),), 1)
    empty = jnp.zeros(
        (frames, latent.shape[1], latent.shape[2], first_kernel.shape[2]), jnp.float32
    )
    inputs = padded
    pre = empty + conv_block(inputs, lax.all_gather(first_kernel, "tm", axis=0, tiled=True))
    hidden = jax.nn.silu(pre).astype(jnp.bfloat16)
    hidden_past = shifted(hidden[frames - 2 :], "tm", 1)
    hidden_ext = jnp.concatenate([hidden_past, hidden], 0)
    larger = padded_2(upsample(hidden_ext), (("space", 1),), 1)
    blank = jnp.zeros(
        (frames, 2 * latent.shape[1], 2 * latent.shape[2], second_kernel.shape[2]), jnp.float32
    )
    piece = lax.all_gather(second_kernel, "tm", axis=0, tiled=True)
    inputs = lax.slice_in_dim(larger, 0, piece.shape[0], axis=3)
    result = blank + conv_block(inputs, piece)
    return result.astype(jnp.bfloat16)


def solution(mesh):
    in_specs = (P(("groups", "tm"), "space", None, None), P("tm", None, None), P("tm", None, None))
    out_specs = P(("groups", "tm"), "space", None, None)
    return jax.shard_map(shards, mesh=mesh, in_specs=in_specs, out_specs=out_specs, check_vma=False)
```

profile of v0, /device:TPU:3, one launch (start us, length us, event | category | flops | bytes accessed | tf_op | source)
XLA Modules:
  0.0 142.4 jit_solution(16999279669549598661)
XLA Ops:
  6.5 0.0 all-gather.3.cloned.1.call-start
  6.5 0.7 all-gather.3.cloned.1.call-update
  7.3 0.0 all-gather.5.cloned.1.call-start
  7.3 0.7 all-gather.5.cloned.1.call-update
  8.0 3.2 %collective-permute-start = (bf16[2,8,32,256]{3,2,1,0:T(8,128)(2,1)}, bf16[2,8,32,256]{3,2,1,0:T(8,128)(2,1)S(1)}, u32[]{:S(2)}, u32[]{:S(2)}) collective-permute-start(bf16[2,8,32,256]{3,2,1,0:T(8,128)(2,1)} %param.3), channel_id=1, source_target_pairs={{0,2},{2,4},{4,6},{6,8},{8,10},{10,12},{12,14},{1,3},{3,5},{5,7},{... | collective-permute-start | bytes 786440 | tf_op jit(solution)/shard_map/ppermute | solution.py:10
  11.2 6.1 %collective-permute-done = bf16[2,8,32,256]{3,2,1,0:T(8,128)(2,1)S(1)} collective-permute-done((bf16[2,8,32,256]{3,2,1,0:T(8,128)(2,1)}, bf16[2,8,32,256]{3,2,1,0:T(8,128)(2,1)S(1)}, u32[]{:S(2)}, u32[]{:S(2)}) %collective-permute-start) | collective-permute-done | bytes 262176 | tf_op jit(solution)/shard_map/ppermute | solution.py:10
  17.3 1.0 constant_dynamic-update-slice_fusion
  18.3 1.3 collective-permute-start.1
  19.6 3.5 %collective-permute-start.2 = (bf16[4,1,32,256]{3,2,1,0:T(8,128)(2,1)S(1)}, bf16[4,1,32,256]{3,2,1,0:T(8,128)(2,1)S(1)}, u32[]{:S(2)}, u32[]{:S(2)}) collective-permute-start(bf16[4,1,32,256]{3,2,1,0:T(8,128)(2,1)S(1)} %get-tuple-element.8), channel_id=1, source_target_pairs={{1,0},{3,2},{5,4},{7,6},{9,8},{11,10},{13,12},{15,14},{17,16},{19,... | collective-permute-start | bytes 196616 | tf_op jit(solution)/shard_map/ppermute | solution.py:21
  23.1 0.0 collective-permute-done.1
  23.1 0.9 collective-permute-done.2
  24.0 0.1 maximum_bitcast_fusion.1
  24.0 0.0 copy-start.1
  24.1 0.5 copy.13
  24.6 0.3 pad.clone
  24.9 0.1 copy.6
  25.0 0.1 slice.22
  25.1 47.7 %all-gather.3.cloned.1.call-done = bf16[256,27,256]{2,0,1:T(8,128)(2,1)} async-done(((bf16[32,27,256]{2,0,1:T(8,128)(2,1)}), bf16[256,27,256]{2,0,1:T(8,128)(2,1)}) %all-gather.3.cloned.1.call-update) | async-done | bytes 3538960 | tf_op jit(solution)/shard_map/all_gather | solution.py:54
  72.8 0.0 copy-done.1
  72.8 4.4 %convolution_select_fusion = f32[2,8,8,5,256]{4,2,3,1,0:T(8,128)S(1)} fusion(bf16[256,3,3,3,256]{4,0,3,2,1:T(8,128)(2,1)} %bitcast.37, bf16[4,10,1,7,2,256]{5,3,4,1,0,2:T(8,128)(2,1)S(1)} %slice.22, bf16[4,10,1,8,5,256]{5,3,4,1,0,2:T(8,128)(2,1)S(1)} %copy.6, pred[8,5]{0,1:T(8,128)(4,1)S(1)} %copy-done.1), kind=kOutput, calls=%fused_computation.14 | convolution fusion | flops 2268528640 | bytes 5300264 | tf_op jit(solution)/shard_map/conv_general_dilated | solution.py:30
  77.3 0.2 copy.7
  77.5 0.1 multiply_convert_fusion
  77.6 4.0 %collective-permute-start.3 = (bf16[2,8,32,256]{3,1,2,0:T(8,128)(2,1)S(1)}, bf16[2,8,32,256]{3,1,2,0:T(8,128)(2,1)S(1)}, u32[]{:S(2)}, u32[]{:S(2)}) collective-permute-start(bf16[2,8,32,256]{3,1,2,0:T(8,128)(2,1)S(1)} %multiply_convert_fusion), channel_id=1, source_target_pairs={{0,2},{2,4},{4,6},{6,8},{8,10},{10,12},{12,14},{1,3},{3,5},{5,7},{... | collective-permute-start | bytes 786440 | tf_op jit(solution)/shard_map/ppermute | solution.py:10
  81.7 3.4 %collective-permute-done.3 = bf16[2,8,32,256]{3,1,2,0:T(8,128)(2,1)S(1)} collective-permute-done((bf16[2,8,32,256]{3,1,2,0:T(8,128)(2,1)S(1)}, bf16[2,8,32,256]{3,1,2,0:T(8,128)(2,1)S(1)}, u32[]{:S(2)}, u32[]{:S(2)}) %collective-permute-start.3) | collective-permute-done | bytes 262176 | tf_op jit(solution)/shard_map/ppermute | solution.py:10
  85.1 0.4 copy.8
  85.6 0.4 broadcast_in_dim.13
  86.0 0.6 broadcast_in_dim.14
  86.6 0.1 fusion.29
  86.7 1.3 collective-permute-start.4
  88.0 7.6 %collective-permute-start.5 = (bf16[4,1,64,256]{3,0,2,1:T(4,128)(2,1)S(1)}, bf16[4,1,64,256]{3,0,2,1:T(4,128)(2,1)S(1)}, u32[]{:S(2)}, u32[]{:S(2)}) collective-permute-start(bf16[4,1,64,256]{3,0,2,1:T(4,128)(2,1)S(1)} %get-tuple-element.6), channel_id=1, source_target_pairs={{1,0},{3,2},{5,4},{7,6},{9,8},{11,10},{13,12},{15,14},{17,16},{19,... | collective-permute-start | bytes 393224 | tf_op jit(solution)/shard_map/ppermute | solution.py:21
  95.6 0.0 collective-permute-done.4
  95.6 0.8 collective-permute-done.5
  96.4 1.8 %maximum_bitcast_fusion = bf16[4,18,1,64,256]{4,0,3,1,2:T(4,128)(2,1)S(1)} fusion(bf16[4,1,64,256]{3,0,2,1:T(4,128)(2,1)S(1)} %collective-permute-done.5, bf16[4,16,64,256]{3,0,2,1:T(4,128)(2,1)S(1)} %bitcast.32, bf16[4,1,64,256]{3,0,2,1:T(4,128)(2,1)S(1)} %collective-permute-done.4), kind=kLoop, calls=%fused_computation.8 | loop fusion | flops 2359296 | bytes 4718592 | tf_op jit(solution)/shard_map/broadcast_in_dim | solution.py:31
  98.2 1.4 pad.2
  99.7 0.0 copy-start
  99.7 0.3 copy.10
  100.0 0.1 slice.26
  100.2 24.4 %all-gather.5.cloned.1.call-done = bf16[256,27,128]{2,0,1:T(8,128)(2,1)} async-done(((bf16[32,27,128]{2,0,1:T(8,128)(2,1)}), bf16[256,27,128]{2,0,1:T(8,128)(2,1)}) %all-gather.5.cloned.1.call-update) | async-done | bytes 1769488 | tf_op jit(solution)/shard_map/all_gather | solution.py:62
  124.6 0.0 copy-done
  124.6 9.9 %fusion.13 = bf16[2,16,8,9,128]{4,2,3,1,0:T(8,128)(2,1)S(1)} fusion(bf16[256,3,3,3,128]{4,0,3,2,1:T(8,128)(2,1)} %bitcast.38, bf16[4,18,1,7,2,256]{5,3,4,1,0,2:T(8,128)(2,1)S(1)} %slice.26, bf16[4,18,1,8,9,256]{5,3,4,1,0,2:T(8,128)(2,1)S(1)} %copy.10, pred[8,9]{0,1:T(8,128)(4,1)S(1)} %copy-done), kind=kOutput, calls=%fused_computation.13 | convolution fusion | flops 4087185408 | bytes 5529672 | tf_op jit(solution)/shard_map/conv_general_dilated | solution.py:30
  134.5 0.1 copy.11
  134.6 0.9 copy.12
  (4 shorter events, 0.1 us)
Async XLA Ops:
  6.5 66.3 %all-gather.3.cloned.1.call-start = ((), (), s32[]{:S(2)}) async-start(), calls=%async_computation | async-start | bytes 3981312 | tf_op jit(solution)/shard_map/all_gather | solution.py:54
  7.3 117.3 %all-gather.5.cloned.1.call-start = ((), (), s32[]{:S(2)}) async-start(), calls=%async_computation.1 | async-start | bytes 1990656 | tf_op jit(solution)/shard_map/all_gather | solution.py:62
  8.0 9.3 %collective-permute-start = (bf16[2,8,32,256]{3,2,1,0:T(8,128)(2,1)}, bf16[2,8,32,256]{3,2,1,0:T(8,128)(2,1)S(1)}, u32[]{:S(2)}, u32[]{:S(2)}) collective-permute-start(bf16[2,8,32,256]{3,2,1,0:T(8,128)(2,1)} %param.3), channel_id=1, source_target_pairs={{0,2},{2,4},{4,6},{6,8},{8,10},{10,12},{12,14},{1,3},{3,5},{5,7},{... | collective-permute-start | bytes 786440 | tf_op jit(solution)/shard_map/ppermute | solution.py:10
  18.3 4.8 %collective-permute-start.1 = (bf16[4,1,32,256]{3,2,1,0:T(8,128)(2,1)S(1)}, bf16[4,1,32,256]{3,2,1,0:T(8,128)(2,1)S(1)}, u32[]{:S(2)}, u32[]{:S(2)}) collective-permute-start(bf16[4,1,32,256]{3,2,1,0:T(8,128)(2,1)S(1)} %get-tuple-element.7), channel_id=1, source_target_pairs={{0,1},{2,3},{4,5},{6,7},{8,9},{10,11},{12,13},{14,15},{16,17},{18,... | collective-permute-start | bytes 196616 | tf_op jit(solution)/shard_map/ppermute | solution.py:20
  19.6 4.3 %collective-permute-start.2 = (bf16[4,1,32,256]{3,2,1,0:T(8,128)(2,1)S(1)}, bf16[4,1,32,256]{3,2,1,0:T(8,128)(2,1)S(1)}, u32[]{:S(2)}, u32[]{:S(2)}) collective-permute-start(bf16[4,1,32,256]{3,2,1,0:T(8,128)(2,1)S(1)} %get-tuple-element.8), channel_id=1, source_target_pairs={{1,0},{3,2},{5,4},{7,6},{9,8},{11,10},{13,12},{15,14},{17,16},{19,... | collective-permute-start | bytes 196616 | tf_op jit(solution)/shard_map/ppermute | solution.py:21
  24.0 48.8 %copy-start.1 = (pred[8,5]{0,1:T(8,128)(4,1)S(1)}, pred[8,5]{0,1:T(8,128)(4,1)}, u32[]{:S(2)}) copy-start(pred[8,5]{0,1:T(8,128)(4,1)} %constant.13) | copy-start | bytes 124
  77.6 7.4 %collective-permute-start.3 = (bf16[2,8,32,256]{3,1,2,0:T(8,128)(2,1)S(1)}, bf16[2,8,32,256]{3,1,2,0:T(8,128)(2,1)S(1)}, u32[]{:S(2)}, u32[]{:S(2)}) collective-permute-start(bf16[2,8,32,256]{3,1,2,0:T(8,128)(2,1)S(1)} %multiply_convert_fusion), channel_id=1, source_target_pairs={{0,2},{2,4},{4,6},{6,8},{8,10},{10,12},{12,14},{1,3},{3,5},{5,7},{... | collective-permute-start | bytes 786440 | tf_op jit(solution)/shard_map/ppermute | solution.py:10
  86.7 8.9 %collective-permute-start.4 = (bf16[4,1,64,256]{3,0,2,1:T(4,128)(2,1)S(1)}, bf16[4,1,64,256]{3,0,2,1:T(4,128)(2,1)S(1)}, u32[]{:S(2)}, u32[]{:S(2)}) collective-permute-start(bf16[4,1,64,256]{3,0,2,1:T(4,128)(2,1)S(1)} %get-tuple-element.5), channel_id=1, source_target_pairs={{0,1},{2,3},{4,5},{6,7},{8,9},{10,11},{12,13},{14,15},{16,17},{18,... | collective-permute-start | bytes 393224 | tf_op jit(solution)/shard_map/ppermute | solution.py:20
  88.0 8.4 %collective-permute-start.5 = (bf16[4,1,64,256]{3,0,2,1:T(4,128)(2,1)S(1)}, bf16[4,1,64,256]{3,0,2,1:T(4,128)(2,1)S(1)}, u32[]{:S(2)}, u32[]{:S(2)}) collective-permute-start(bf16[4,1,64,256]{3,0,2,1:T(4,128)(2,1)S(1)} %get-tuple-element.6), channel_id=1, source_target_pairs={{1,0},{3,2},{5,4},{7,6},{9,8},{11,10},{13,12},{15,14},{17,16},{19,... | collective-permute-start | bytes 393224 | tf_op jit(solution)/shard_map/ppermute | solution.py:21
  99.7 24.9 %copy-start = (pred[8,9]{0,1:T(8,128)(4,1)S(1)}, pred[8,9]{0,1:T(8,128)(4,1)}, u32[]{:S(2)}) copy-start(pred[8,9]{0,1:T(8,128)(4,1)} %constant.12) | copy-start | bytes 220
Sparse Core Ops, SparseCore 0:
  9.5 63.2 all-gather.2
  74.9 49.6 all-gather.4
where the time goes:
time: 144 us; the launch traced here: 142 us
  waiting for transfers between devices  84.7 us (59%)
  starting transfers between devices  20.9 us (15%)
  matrix products  14.4 us (10%)
  between operations  13.6 us (9%)
  local copies, waits for them, and re-layouts  6.71 us (5%)
  other arithmetic  2.09 us (1%)
    all_gather x1, waiting for transfers between devices, shards(): lax.all_gather(first_kernel, 'tm', axis=0, tiled=True)  47.7 us
    all_gather x1, waiting for transfers between devices, shards(): piece = lax.all_gather(second_kernel, 'tm', axis=0, tiled=True)  24.4 us
    conv_general_dilated x2, matrix products, conv_block(): lax.conv_general_dilated(padded[None], filters, (1, 1, 1), ((0, 0), (0, 0...  14.4 us
    ppermute x2, starting transfers between devices, padded_2(): after = lax.ppermute(leading, axis, down)  11.1 us
    ppermute x2, waiting for transfers between devices, shifted(): return lax.ppermute(x, axis, pairs)  9.51 us
    ppermute x2, starting transfers between devices, shifted(): return lax.ppermute(x, axis, pairs)  7.22 us
  transfers between devices with their start and end apart: 8, of which 6 were waited for; matrix products, arithmetic and copies ran while one was open for 9% of the time, Pallas kernels for 0%

commit v1 on v0

v1 whole, which is shorter than its diff:
```python
import functools

import jax
import jax.numpy as jnp
from jax import lax
from jax.experimental import pallas as pl
from jax.experimental.pallas import tpu as pltpu
from jax.sharding import PartitionSpec as P

MESH = pl.DeviceIdType.MESH
F32 = jnp.float32
BF16 = jnp.bfloat16


def shifted(x, axis, by):
    count = lax.axis_size(axis)
    pairs = [(i, i + by) for i in range(count) if 0 <= i + by < count]
    return lax.ppermute(x, axis, pairs)


def padded_2(x, sides, width):
    for axis, dim in sides:
        count, length = (lax.axis_size(axis), x.shape[dim])
        up = [(i, (i + 1) % count) for i in range(count - 1)]
        down = [(j, i) for i, j in up]
        last = lax.slice_in_dim(x, length - width, length, axis=dim)
        leading = lax.slice_in_dim(x, 0, width, axis=dim)
        before = lax.ppermute(last, axis, up)
        after = lax.ppermute(leading, axis, down)
        x = jnp.concatenate([before, x, after], axis=dim)
    return x


def conv_block(padded, kernel):
    channels = kernel.shape[0]
    outputs = kernel.shape[2]
    filters = kernel.reshape(channels, 3, 3, 3, outputs).transpose(1, 2, 3, 0, 4)
    result = lax.conv_general_dilated(
        padded[None],
        filters,
        (1, 1, 1),
        ((0, 0), (0, 0), (1, 1)),
        dimension_numbers=("NDHWC", "DHWIO", "NDHWC"),
        preferred_element_type=jnp.float32,
    )
    return result[0]


def upsample(field):
    return jnp.repeat(jnp.repeat(field, 2, axis=1), 2, axis=2)


def plain(latent, first_kernel, second_kernel):
    frames = latent.shape[0]
    extended = jnp.concatenate([shifted(latent[frames - 2 :], "tm", 1), latent], 0)
    padded = padded_2(extended, (("space", 1),), 1)
    pre = conv_block(padded, lax.all_gather(first_kernel, "tm", axis=0, tiled=True))
    hidden = jax.nn.silu(pre).astype(BF16)
    hidden_ext = jnp.concatenate([shifted(hidden[frames - 2 :], "tm", 1), hidden], 0)
    larger = padded_2(upsample(hidden_ext), (("space", 1),), 1)
    piece = lax.all_gather(second_kernel, "tm", axis=0, tiled=True)
    return conv_block(larger, piece).astype(BF16)


def roll_cols(x, by, width):
    rows = x.shape[0]
    col = lax.broadcasted_iota(jnp.int32, x.shape, 0) % width
    if by == 1:
        return jnp.where(col == 0, 0.0, pltpu.roll(x, 1, 0))
    return jnp.where(col == width - 1, 0.0, pltpu.roll(x, rows - 1, 0))


def kernel(
    n, latent, k1, k2, out,
    b1, b2, x, h, v, acc, wide,
    own_sem, lat_send, lat_recv, hid_send, hid_recv,
    ring1, ring2, yrec1, yrec2, ring_send, y_send, sib_send, sibf_send, sib1, sib2, sibf1, sibf2,
):
    y = lax.axis_index("groups")
    tm = lax.axis_index("tm")
    c = lax.axis_index("space")
    half = n // 2
    rows, width, c1 = latent.shape[1:]
    c2 = k2.shape[2]
    m = rows * width

    odd = tm % 2
    pos = (1 - odd) * (tm // 2) + odd * (n - 1 - tm // 2)

    def at(p):
        q = (p + 2 * n) % n
        u = q // half
        return (1 - u) * (2 * q) + u * (2 * (n - 1 - q) + 1)

    ring_to = [(y, at(pos + 1), c), (y, at(pos - 1), c)]
    sibling = (y, tm, 1 - c)
    across = (1 - y, tm, c)
    after = (tm + 1) % n
    before = (tm + n - 1) % n

    barrier = pltpu.get_barrier_semaphore()
    partners = ring_to + [sibling, across, (y, after, c), (y, after, 1 - c), (y, before, c), (y, before, 1 - c)]
    for d in partners:
        pl.semaphore_signal(barrier, inc=1, device_id=d, device_id_type=MESH)

    third = 2 * y * (1 - c) + c
    other = 2 * (1 - y)

    def rcopy(src, dst, ss, rs, dev):
        return pltpu.make_async_remote_copy(
            src_ref=src, dst_ref=dst, send_sem=ss, recv_sem=rs, device_id=dev, device_id_type=MESH
        )

    def drain(ref, sem):
        pltpu.make_async_copy(ref, ref, sem).wait()

    own = [
        pltpu.make_async_copy(k1, b1.at[tm], own_sem.at[0]),
        pltpu.make_async_copy(k2, b2.at[tm], own_sem.at[1]),
        pltpu.make_async_copy(latent, x.at[2:4, 1:9], own_sem.at[2]),
    ]
    for o in own:
        o.start()
    zline = jnp.zeros((4, 1, width, c1), BF16)
    x[:, pl.ds(9 * c, 1)] = zline
    h[:, pl.ds(9 * c, 1)] = zline

    @pl.when(tm == 0)
    def _():
        x[0:2] = jnp.zeros((2, 10, width, c1), BF16)
        h[0:2] = jnp.zeros((2, 10, width, c1), BF16)

    pl.semaphore_wait(barrier, len(partners))

    class Gather:
        def __init__(self, src, buf, ring, yrec, sib, sibf, cuts, far, which):
            self.src, self.buf, self.ring, self.yrec = src, buf, ring, yrec
            self.sib, self.sibf, self.cuts, self.far, self.which = sib, sibf, cuts, far, which
            self.size = 9 // cuts

        def taps(self, t, j):
            return pl.ds(t * 9 + self.size * j, self.size)

        def send_own(self):
            for j in range(self.cuts):
                for d in range(2):
                    if self.far[d] >= 1:
                        t = self.taps(third, j)
                        rcopy(self.src.at[t], self.buf.at[tm, t], ring_send.at[self.which], self.ring.at[d, 0, j], ring_to[d]).start()

        def shard(self, d, k):
            return at(pos - k) if d == 0 else at(pos + k)

        def ring_step(self, k):
            for j in range(self.cuts):
                for d in range(2):
                    if k > self.far[d]:
                        continue
                    s = self.shard(d, k)
                    r = self.buf.at[s, self.taps(third, j)]
                    drain(r, self.ring.at[d, k - 1, j])
                    if k < self.far[d]:
                        rcopy(r, r, ring_send.at[self.which], self.ring.at[d, k, j], ring_to[d]).start()
                    rcopy(r, r, sib_send.at[self.which], self.sib, sibling).start()

                    @pl.when(c == 0)
                    def _():
                        rcopy(r, r, y_send.at[self.which], self.yrec.at[d, k - 1, j], across).start()

        def y_step(self, k):
            @pl.when(c == 0)
            def _():
                for j in range(self.cuts):
                    for d in range(2):
                        if k > self.far[d]:
                            continue
                        r = self.buf.at[self.shard(d, k), self.taps(other, j)]
                        drain(r, self.yrec.at[d, k - 1, j])
                        rcopy(r, r, sibf_send.at[self.which], self.sibf, sibling).start()

        def arrive(self):
            drain(self.buf.at[0 : n - 1, 0:9], self.sib)

            @pl.when(c == 1)
            def _():
                drain(self.buf.at[0 : n - 1, 0:9], self.sibf)

        def finish(self):
            ref = self.buf.at[0 : n - 1, 0:9]
            drain(ref, ring_send.at[self.which])
            drain(ref, sib_send.at[self.which])

            @pl.when(c == 0)
            def _():
                drain(ref, y_send.at[self.which])
                drain(ref, sibf_send.at[self.which])

    far = half
    g1 = Gather(k1, b1, ring1, yrec1, sib1, sibf1, 3, (far, n - 1 - far), 0)
    g2 = Gather(k2, b2, ring2, yrec2, sib2, sibf2, 1, (n - 1 - far, far), 1)

    def halo(src, edge, dst, ss, rs, frame):
        f = pl.ds(frame, 1)
        line = pl.ds(9 * c, 1)
        ahead = rcopy(src, dst.at[f, 1:9], ss.at[0, frame], rs.at[0, frame], (y, after, c))
        cross = rcopy(edge, dst.at[pl.ds(frame + 2, 1), line], ss.at[1, frame], rs.at[1, frame], sibling)
        both = rcopy(edge, dst.at[f, line], ss.at[2, frame], rs.at[2, frame], (y, after, 1 - c))
        return ahead, cross, both

    def start_halo(copies):
        ahead, cross, both = copies
        cross.start()

        @pl.when(tm < n - 1)
        def _():
            ahead.start()
            both.start()

    def recv_time(copies):
        ahead, cross, both = copies

        @pl.when(tm > 0)
        def _():
            ahead.wait_recv()

    lat = [halo(latent.at[f : f + 1], latent.at[f : f + 1, pl.ds(7 - 7 * c, 1)], x, lat_send, lat_recv, f) for f in range(2)]
    hid = [halo(h.at[f + 2 : f + 3, 1:9], h.at[f + 2 : f + 3, pl.ds(8 - 7 * c, 1)], h, hid_send, hid_recv, f) for f in range(2)]
    mine = pl.ds(9 - 9 * c, 1)

    def recv_both(dst, rs, frame):
        @pl.when(tm > 0)
        def _():
            drain(dst.at[frame : frame + 1, 1:9], rs.at[0, frame])
            drain(dst.at[frame : frame + 1, mine], rs.at[2, frame])

    def recv_cross(dst, rs, frame):
        drain(dst.at[frame + 2 : frame + 3, mine], rs.at[1, frame])

    g1.send_own()
    for f in range(2):
        start_halo(lat[f])
    for k in range(1, far + 1):
        if k == far:
            g2.send_own()
        g1.ring_step(k)
        if k > 1:
            g1.y_step(k - 1)
    g2.ring_step(1)
    g1.y_step(far)
    for o in own:
        o.wait()
    g1.arrive()
    for f in range(2):
        recv_both(x, lat_recv, f)
        recv_cross(x, lat_recv, f)

    def slab(ref, f, r):
        return ref[f, r : r + 8].reshape(m, c1)

    def weight(dt, dr, dc):
        return b1[:, 9 * dt + 3 * dr + dc].reshape(c1, b1.shape[3])

    def conv1(f):
        lhs = jnp.concatenate([slab(x, f + dt, dr) for dt in range(3) for dr in range(3)], axis=1)
        parts = []
        for dc in range(3):
            rhs = jnp.concatenate([weight(dt, dr, dc) for dt in range(3) for dr in range(3)], axis=0)
            parts.append(jnp.dot(lhs, rhs, preferred_element_type=F32))
        pre = roll_cols(parts[0], 1, width) + parts[1] + roll_cols(parts[2], -1, width)
        val = pre / (1.0 + jnp.exp(-pre))
        h[f + 2, 1:9] = val.astype(BF16).reshape(rows, width, c1)

    conv1(0)
    start_halo(hid[0])
    g2.ring_step(2)
    g2.y_step(1)
    conv1(1)
    start_halo(hid[1])
    for k in range(3, far + 1):
        g2.ring_step(k)
        g2.y_step(k - 1)
    g2.y_step(far)
    g2.arrive()

    for dt in range(3):
        w = [[b2[:, 9 * dt + 3 * dr + dc].reshape(c1, c2).astype(F32) for dc in range(3)] for dr in range(3)]
        lines = [
            [w[0], [w[1][i] + w[2][i] for i in range(3)]],
            [[w[0][i] + w[1][i] for i in range(3)], w[2]],
        ]
        for pr in range(2):
            for ro in range(2):
                a = lines[pr][ro]
                v[pr, 2 * dt + ro] = jnp.concatenate([a[0], a[2], a[1] + a[2], a[0] + a[1]], axis=1).astype(BF16)

    def term(f, pr, dts):
        lhs = jnp.concatenate([slab(h, f + dt, pr + ro) for dt in dts for ro in range(2)], axis=1)
        rhs = v[pr, 2 * dts[0] : 2 * dts[-1] + 2].reshape(2 * len(dts) * c1, 4 * c2)
        return jnp.dot(lhs, rhs, preferred_element_type=F32)

    for f in range(2):
        recv_cross(h, hid_recv, f)
    early = [(2,), (1, 2)]
    late = [(0, 1), (0,)]
    for f in range(2):
        for pr in range(2):
            acc[f, pr] = term(f, pr, early[f])
    for f in range(2):
        recv_both(h, hid_recv, f)
    for f in range(2):
        for pr in range(2):
            p = acc[f, pr] + term(f, pr, late[f])
            left = roll_cols(p[:, 0:c2], 1, width) + p[:, 2 * c2 : 3 * c2]
            right = p[:, 3 * c2 : 4 * c2] + roll_cols(p[:, c2 : 2 * c2], -1, width)
            wide[pl.ds(0, m, stride=2)] = left
            wide[pl.ds(1, m, stride=2)] = right
            res = wide[...].astype(BF16).reshape(rows, 2 * width, c2)
            for r in range(rows):
                out[f, 2 * r + pr] = res[r]

    g1.finish()
    g2.finish()
    for copies in lat + hid:
        ahead, cross, both = copies
        cross.wait_send()

        @pl.when(tm < n - 1)
        def _():
            ahead.wait_send()
            both.wait_send()


def fused(n, latent, first_kernel, second_kernel):
    frames, rows, width, c1 = latent.shape
    ch, _, o1 = first_kernel.shape
    c2 = second_kernel.shape[2]
    k1 = first_kernel.transpose(1, 0, 2)
    k2 = second_kernel.transpose(1, 0, 2)
    far = n // 2
    dma = pltpu.SemaphoreType.DMA
    vm = pl.BlockSpec(memory_space=pltpu.VMEM)
    m = rows * width
    return pl.pallas_call(
        functools.partial(kernel, n),
        out_shape=jax.ShapeDtypeStruct((frames, 2 * rows, 2 * width, c2), BF16),
        in_specs=[vm] * 3,
        out_specs=vm,
        scratch_shapes=[
            pltpu.VMEM((n, 27, ch, o1), BF16),
            pltpu.VMEM((n, 27, ch, c2), BF16),
            pltpu.VMEM((4, rows + 2, width, c1), BF16),
            pltpu.VMEM((4, rows + 2, width, o1), BF16),
            pltpu.VMEM((2, 6, o1, 4 * c2), BF16),
            pltpu.VMEM((2, 2, m, 4 * c2), F32),
            pltpu.VMEM((2 * m, c2), F32),
            dma((3,)), dma((3, 2)), dma((3, 2)), dma((3, 2)), dma((3, 2)),
            dma((2, far, 3)), dma((2, far, 1)), dma((2, far, 3)), dma((2, far, 1)),
            dma((2,)), dma((2,)), dma((2,)), dma((2,)), dma, dma, dma, dma,
        ],
        compiler_params=pltpu.CompilerParams(
            collective_id=0, has_side_effects=True, vmem_limit_bytes=58 * 1024 * 1024
        ),
    )(latent, k1, k2)


def solution(mesh):
    n = mesh.shape["tm"]

    def shards(latent, first_kernel, second_kernel):
        ch = first_kernel.shape[0]
        fits = (
            ch % 16 == 0 and n % 2 == 0 and n >= 4 and latent.shape[:2] == (2, 8)
            and mesh.shape["space"] == 2 and mesh.shape["groups"] == 2
        )
        if fits:
            return fused(n, latent, first_kernel, second_kernel)
        return plain(latent, first_kernel, second_kernel)

    in_specs = (P(("groups", "tm"), "space", None, None), P("tm", None, None), P("tm", None, None))
    out_specs = P(("groups", "tm"), "space", None, None)
    return jax.shard_map(shards, mesh=mesh, in_specs=in_specs, out_specs=out_specs, check_vma=False)
```

time: 144 us -> 52.8 us (0.37); the launches traced: 142 us -> 52.7 us
  waiting for transfers between devices: 84.7 us -> 0 us
  Pallas kernels: 0 us -> 50.8 us
  starting transfers between devices: 20.9 us -> 0 us
  matrix products: 14.4 us -> 0 us
  between operations: 13.6 us -> 0.01 us
  local copies, waits for them, and re-layouts: 6.71 us -> 1.87 us
  other arithmetic: 2.09 us -> 0 us
    all_gather x2 -> x0, waiting for transfers between devices: 72.1 us -> none  [the longest x1 47.7 us: shards(): lax.all_gather(first_kernel, 'tm', axis=0, tiled=True)]
    pallas_call x0 -> x1, Pallas kernels: none -> 50.8 us  [fused(): pl.pallas_call(functools.partial(kernel, n), out_shape=jax.ShapeDtypeStru...]
    ppermute x6 -> x0, starting transfers between devices: 20.9 us -> none  [the longest x2 11.1 us: padded_2(): after = lax.ppermute(leading, axis, down)]
    conv_general_dilated x2 -> x0, matrix products: 14.4 us -> none  [conv_block(): lax.conv_general_dilated(padded[None], filters, (1, 1, 1), ((0, 0), (0, 0...]
    ppermute x6 -> x0, waiting for transfers between devices: 11.2 us -> none  [the longest x2 9.51 us: shifted(): return lax.ppermute(x, axis, pairs)]
    broadcast_in_dim x4 -> x0, local copies, waits for them, and re-layouts: 2.76 us -> none  [the longest x2 1.74 us: conv_block(): padded[None]]
    broadcast_in_dim x2 -> x0, other arithmetic: 1.89 us -> none  [conv_block(): padded[None]]
  transfers between devices with their start and end apart: 8 -> 0, of which waited for: 6 -> 0; matrix products, arithmetic and copies ran while one was open for 9% -> 0% of each run, Pallas kernels for 0% -> 0%
where the time goes in v1:
time: 52.8 us; the launch traced here: 52.7 us
  Pallas kernels  50.8 us (96%)
  local copies, waits for them, and re-layouts  1.87 us (4%)
    pallas_call x1, Pallas kernels, fused(): pl.pallas_call(functools.partial(kernel, n), out_shape=jax.ShapeDtypeStru...  50.8 us
    unnamed x1, local copies, waits for them, and re-layouts  1.87 us

profile of v1, /device:TPU:3, one launch (start us, length us, event | category | flops | bytes accessed | tf_op | source)
XLA Modules:
  0.0 52.7 jit_solution(18259307414991947694)
XLA Ops:
  0.0 50.8 %shard_map.37 = bf16[2,16,64,128]{3,2,1,0:T(8,128)(2,1)} custom-call(bf16[2,8,32,256]{3,2,1,0:T(8,128)(2,1)} %latent.1, bf16[27,32,256]{2,1,0:T(8,128)(2,1)} %bitcast.2, bf16[27,32,128]{2,1,0:T(8,128)(2,1)} %bitcast.3), custom_call_target="tpu_custom_call" | custom-call | tf_op jit(solution)/shard_map/pallas_call | solution.py:343
  50.8 1.9 %copy.5 = bf16[2,16,64,128]{3,2,1,0:T(8,128)(2,1)} copy(bf16[2,16,64,128]{3,2,1,0:T(8,128)(2,1)} %shard_map.37) | data formatting | bytes 1048576

commit v2 on v1

--- a/solution.py
+++ b/solution.py
@@ -197,7 +197,7 @@
 
     far = half
     g1 = Gather(k1, b1, ring1, yrec1, sib1, sibf1, 3, (far, n - 1 - far), 0)
-    g2 = Gather(k2, b2, ring2, yrec2, sib2, sibf2, 1, (n - 1 - far, far), 1)
+    g2 = Gather(k2, b2, ring2, yrec2, sib2, sibf2, 3, (n - 1 - far, far), 1)
 
     def halo(src, edge, dst, ss, rs, frame):
         f = pl.ds(frame, 1)
@@ -354,7 +354,7 @@
             pltpu.VMEM((2, 2, m, 4 * c2), F32),
             pltpu.VMEM((2 * m, c2), F32),
             dma((3,)), dma((3, 2)), dma((3, 2)), dma((3, 2)), dma((3, 2)),
-            dma((2, far, 3)), dma((2, far, 1)), dma((2, far, 3)), dma((2, far, 1)),
+            dma((2, far, 3)), dma((2, far, 3)), dma((2, far, 3)), dma((2, far, 3)),
             dma((2,)), dma((2,)), dma((2,)), dma((2,)), dma, dma, dma, dma,
         ],
         compiler_params=pltpu.CompilerParams(

time: 52.8 us -> 52.6 us (level)
  no operation moved by 1% of the time
where the time goes in v2:
time: 52.6 us; the launch traced here: 52.4 us
  Pallas kernels  50.5 us (96%)
  local copies, waits for them, and re-layouts  1.87 us (4%)
    pallas_call x1, Pallas kernels, fused(): pl.pallas_call(functools.partial(kernel, n), out_shape=jax.ShapeDtypeStru...  50.5 us
    unnamed x1, local copies, waits for them, and re-layouts  1.87 us

profile of v2, /device:TPU:3, one launch (start us, length us, event | category | flops | bytes accessed | tf_op | source)
XLA Modules:
  0.0 52.4 jit_solution(14303703925052063078)
XLA Ops:
  0.0 50.5 %shard_map.37 = bf16[2,16,64,128]{3,2,1,0:T(8,128)(2,1)} custom-call(bf16[2,8,32,256]{3,2,1,0:T(8,128)(2,1)} %latent.1, bf16[27,32,256]{2,1,0:T(8,128)(2,1)} %bitcast.2, bf16[27,32,128]{2,1,0:T(8,128)(2,1)} %bitcast.3), custom_call_target="tpu_custom_call" | custom-call | tf_op jit(solution)/shard_map/pallas_call | solution.py:343
  50.5 1.9 %copy.5 = bf16[2,16,64,128]{3,2,1,0:T(8,128)(2,1)} copy(bf16[2,16,64,128]{3,2,1,0:T(8,128)(2,1)} %shard_map.37) | data formatting | bytes 1048576
